TPU v7x, 256 devices: a whole 4x4x8 slice. The times are simulated.
256 devices in a mesh: dp: 8 (over y_lo, x), lon: 32 (over y_hi, z, core).
Axes of the slice: x: 4, y: 4 (y_hi: 2, y_lo: 2; y = y_hi * 2 + y_lo), z: 8, core: 2. Of those that a mesh axis runs over, the one named last changes fastest.
Arguments:
- fields: bfloat16 [8, 64, 512, 384], P('dp', None, 'lon'), may hold values from -6 to 6
- cotangent: bfloat16 [8, 64, 512, 384], P('dp', None, 'lon'), may hold values from -6 to 6
- kernel_first: bfloat16 [3, 3, 64, 64], replicated, may hold values from -0.25 to 0.25
- kernel_second: bfloat16 [3, 3, 64, 64], replicated, may hold values from -0.25 to 0.25
- metric: float32 [384], replicated, may hold values from 0.5 to 3
Outputs:
- field_grad: bfloat16 [8, 64, 512, 384], P('dp', None, 'lon')
- grad_first: bfloat16 [3, 3, 64, 64], replicated
- grad_second: bfloat16 [3, 3, 64, 64], replicated
All inputs are finite; a program needn't handle non-finite values.
Results may differ from a plain program's by a relative error of at most 0.0063.
Values may be sent and summed in bfloat16 or wider, within the bound.
A program may use at most 64 MiB of HBM per device.

v0:
```python
import jax
import jax.numpy as jnp
from jax import lax
from jax.sharding import PartitionSpec as P

gelu_coef = 0.7978845608


def extended(shard, sides, width):
    for axis, dim in sides:
        count, length = (lax.axis_size(axis), shard.shape[dim])
        up = [(i, (i + 1) % count) for i in range(count)]
        down = [(j, i) for i, j in up]
        last = lax.slice_in_dim(shard, length - width, length, axis=dim)
        first = lax.slice_in_dim(shard, 0, width, axis=dim)
        before = lax.ppermute(last, axis, up)
        after = lax.ppermute(first, axis, down)
        shard = jnp.concatenate([before, shard, after], axis=dim)
    return shard


def gelu_value(u):
    inner = jnp.tanh(gelu_coef * (u + 0.044715 * u * u * u))
    return 0.5 * u * (1.0 + inner)


def gelu_slope(u):
    inner = jnp.tanh(gelu_coef * (u + 0.044715 * u * u * u))
    return 0.5 * (1.0 + inner) + 0.5 * u * (1.0 - inner * inner) * gelu_coef * (
        1.0 + 3.0 * 0.044715 * u * u
    )


def pad_rows(value):
    return jnp.pad(value, ((0, 0), (0, 0), (0, 0), (1, 1)))


def stencil_apply(padded, taps, metric):
    columns = padded.shape[2] - 2
    lat_rows = padded.shape[3] - 2
    total = None
    for p in range(3):
        summed = None
        for q in range(3):
            term = jnp.einsum(
                "oc,bcij->boij",
                taps[p, q],
                padded[:, :, p : p + columns, q : q + lat_rows],
                preferred_element_type=jnp.float32,
            )
            summed = term if summed is None else summed + term
        summed = summed if p == 1 else summed * metric[None, None, None, :]
        total = summed if total is None else total + summed
    return total


def stencil_adjoint(plain_pad, scaled_pad, taps):
    columns = plain_pad.shape[2] - 2
    lat_rows = plain_pad.shape[3] - 2
    total = None
    for p in range(3):
        source = plain_pad if p == 1 else scaled_pad
        for q in range(3):
            term = jnp.einsum(
                "oc,boij->bcij",
                taps[p, q],
                source[:, :, 2 - p : 2 - p + columns, 2 - q : 2 - q + lat_rows],
                preferred_element_type=jnp.float32,
            )
            total = term if total is None else total + term
    return total


def kernel_term(plain, scaled, padded):
    columns = plain.shape[2]
    lat_rows = plain.shape[3]
    terms = []
    for p in range(3):
        source = plain if p == 1 else scaled
        row_terms = []
        for q in range(3):
            row_terms.append(
                jnp.einsum(
                    "boij,bcij->oc",
                    source,
                    padded[:, :, p : p + columns, q : q + lat_rows],
                    preferred_element_type=jnp.float32,
                )
            )
        terms.append(jnp.stack(row_terms))
    return jnp.stack(terms)


def per_device(fields, cotangent, kernel_first, kernel_second, metric):
    metric_padded = jnp.pad(metric, (1, 1))[None, None, None, :]
    samples_here = fields.shape[0]
    stacked = jnp.concatenate((fields, cotangent), axis=0)
    both_pad = extended(stacked, (("lon", 2),), 1)
    input_pad = pad_rows(both_pad[:samples_here])
    upstream_pad = pad_rows(both_pad[samples_here:])
    before_gelu = stencil_apply(input_pad, kernel_first, metric)
    hidden = gelu_value(before_gelu).astype(jnp.bfloat16)
    hidden_pad = pad_rows(extended(hidden, (("lon", 2),), 1))
    scaled_pad = (metric_padded * upstream_pad.astype(jnp.float32)).astype(jnp.bfloat16)
    second = kernel_term(cotangent, scaled_pad[:, :, 1:-1, 1:-1], hidden_pad)
    hidden_grad = stencil_adjoint(upstream_pad, scaled_pad, kernel_second)
    delta = (hidden_grad * gelu_slope(before_gelu)).astype(jnp.bfloat16)
    delta_pad = pad_rows(extended(delta, (("lon", 2),), 1))
    delta_scaled = (metric_padded * delta_pad.astype(jnp.float32)).astype(jnp.bfloat16)
    field_grad = (
        cotangent.astype(jnp.float32) + stencil_adjoint(delta_pad, delta_scaled, kernel_first)
    ).astype(jnp.bfloat16)
    first = kernel_term(delta, delta_scaled[:, :, 1:-1, 1:-1], input_pad)
    first, second = lax.psum((first, second), ("dp", "lon"))
    counted = (
        float(fields.shape[0] * lax.axis_size("dp"))
        * float(fields.shape[2] * lax.axis_size("lon"))
        * float(fields.shape[3])
    )
    factor = jnp.float32(1.0 / counted**0.5)
    return (
        field_grad,
        (first * factor).astype(jnp.bfloat16),
        (second * factor).astype(jnp.bfloat16),
    )


def solution(mesh):
    placed = (P("dp", None, "lon", None), P("dp", None, "lon", None), P(), P(), P())
    return jax.shard_map(
        per_device,
        mesh=mesh,
        in_specs=placed,
        out_specs=(P("dp", None, "lon", None), P(), P()),
        check_vma=False,
    )
```

profile of v0, /device:TPU:1, one launch (start us, length us, event | category | flops | bytes accessed | tf_op | source)
XLA Modules:
  0.0 325.4 jit_solution(10439744815576890022)
XLA Ops:
  7.2 1.4 copy_dynamic-update-slice_fusion
  9.0 3.1 collective-permute-start
  13.7 2.4 collective-permute-done.1
  16.6 0.4 fusion.53
  17.0 0.4 fusion.56
  17.5 0.4 fusion.59
  17.9 0.4 fusion.62
  18.3 0.4 fusion.65
  18.8 0.4 fusion.68
  19.6 1.2 multiply_convert_fusion.2
  21.1 0.6 multiply_convert_fusion.1
  21.7 0.4 fusion.38
  22.2 0.4 fusion.39
  23.0 0.4 fusion.41
  23.5 0.4 fusion.42
  24.4 0.4 fusion.15
  24.8 1.6 fusion.7
  28.1 4.7 %collective-permute-start.5 = (bf16[1,64,1,384]{3,1,2,0:T(8,128)(2,1)S(1)}, bf16[1,64,1,384]{3,1,2,0:T(8,128)(2,1)S(1)}, u32[]{:S(2)}, u32[]{:S(2)}) collective-permute-start(bf16[1,64,1,384]{3,1,2,0:T(8,128)(2,1)S(1)} %get-tuple-element.15), channel_id=1, source_target_pairs={{1,0},{2,1},{3,2},{4,3},{5,4},{6,5},{7,6},{8,7},{9,8},{10,9},{11,1... | collective-permute-start | bytes 147464 | tf_op jit(solution)/shard_map/ppermute | solution.py:17
  32.9 5.4 %collective-permute-start.3 = (bf16[1,64,1,384]{3,1,2,0:T(8,128)(2,1)S(1)}, bf16[1,64,1,384]{3,1,2,0:T(8,128)(2,1)S(1)}, u32[]{:S(2)}, u32[]{:S(2)}) collective-permute-start(bf16[1,64,1,384]{3,1,2,0:T(8,128)(2,1)S(1)} %get-tuple-element.17), channel_id=1, source_target_pairs={{1,0},{2,1},{3,2},{4,3},{5,4},{6,5},{7,6},{8,7},{9,8},{10,9},{11,1... | collective-permute-start | bytes 147464 | tf_op jit(solution)/shard_map/ppermute | solution.py:17
  38.3 0.7 select_maximum_fusion
  39.0 0.5 convolution_bitcast_fusion.3
  39.9 0.4 convolution_bitcast_fusion.2
  40.3 0.7 convolution_bitcast_fusion
  41.0 0.4 convolution_bitcast_fusion.8
  41.5 0.7 convolution_bitcast_fusion.6
  42.2 0.9 multiply_convert_fusion
  43.1 0.7 convolution_bitcast_fusion.11
  43.8 0.7 convolution_bitcast_fusion.15
  44.5 0.7 convolution_bitcast_fusion.17
  45.2 0.7 convolution_bitcast_fusion.9
  45.9 1.6 fusion.29
  47.5 1.6 fusion.30
  49.1 1.6 fusion.31
  50.7 1.7 fusion.32
  52.4 1.6 fusion.33
  53.9 1.6 fusion.34
  55.5 1.7 fusion.35
  57.3 0.5 convolution_bitcast_fusion.1
  57.8 0.5 convolution_bitcast_fusion.7
  58.3 0.8 pad_maximum_fusion.6
  59.0 0.5 convolution_bitcast_fusion.10
  59.5 0.5 convolution_bitcast_fusion.16
  60.0 0.7 pad_maximum_fusion.5
  60.8 5.4 %fusion.8 = bf16[1,64,16,384]{3,1,2,0:T(8,128)(2,1)S(1)} fusion(f32[16,384,64]{1,2,0:T(8,128)} %fusion.29, f32[16,384,64]{1,2,0:T(8,128)} %fusion.30, f32[16,384,64]{1,2,0:T(8,128)} %fusion.31, f32[16,384,64]{1,2,0:T(8,128)S(1)} %fusion.47, f32[16,384,64]{1,2,0:T(8,128)} %fusion.32, f32[16,384,64]{1,2,0:T(8,128)} %fusion.33, f32[16,384,64]{1,2,0:T(8,128)} %fusion.35, ...), kind=kOutput, calls=%fused_computation.16 | convolution fusion | flops 54657024 | bytes 14958592 | tf_op jit(solution)/shard_map/oc,boij->bcij/dot_general | solution.py:64
  66.2 1.3 copy.38
  67.5 247.8 %all-reduce.8.cloned.1.call-done = (f32[3,3,64,64]{3,2,1,0:T(8,128)}, f32[3,3,64,64]{3,2,1,0:T(8,128)}) async-done(((f32[3,3,64,64]{3,2,1,0:T(8,128)}, f32[3,3,64,64]{3,2,1,0:T(8,128)}), (f32[3,3,64,64]{3,2,1,0:T(8,128)}, f32[3,3,64,64]{3,2,1,0:T(8,128)})) %all-reduce.8.cloned.1.call-update) | async-done | bytes 294928 | tf_op jit(solution)/shard_map/psum | solution.py:114
  315.2 1.7 multiply_convert_fusion.3
  316.9 1.7 multiply_convert_fusion.4
  (44 shorter events, 6.1 us)
Async XLA Ops:
  7.2 5.2 %copy-start.1 = (bf16[1,64,16,384]{3,2,1,0:T(8,128)(2,1)S(1)}, bf16[1,64,16,384]{3,2,1,0:T(8,128)(2,1)}, u32[]{:S(2)}) copy-start(bf16[1,64,16,384]{3,2,1,0:T(8,128)(2,1)} %param.5) | copy-start | bytes 2359300
  7.2 1.5 copy-start
  7.2 5.2 %copy-start.2 = (bf16[3,3,64,64]{3,2,1,0:T(8,128)(2,1)S(1)}, bf16[3,3,64,64]{3,2,1,0:T(8,128)(2,1)}, u32[]{:S(2)}) copy-start(bf16[3,3,64,64]{3,2,1,0:T(8,128)(2,1)} %param.7) | copy-start | bytes 221188
  7.2 308.1 %all-reduce.8.cloned.1.call-start = ((), (), s32[]{:S(2)}) async-start(), calls=%async_computation | async-start | bytes 1179648 | tf_op jit(solution)/shard_map/psum | solution.py:114
  8.9 3.8 %copy-start.4 = (bf16[3,3,64,64]{3,2,1,0:T(8,128)(2,1)S(1)}, bf16[3,3,64,64]{3,2,1,0:T(8,128)(2,1)}, u32[]{:S(2)}) copy-start(bf16[3,3,64,64]{3,2,1,0:T(8,128)(2,1)} %param.8) | copy-start | bytes 221188
  9.0 4.7 %collective-permute-start = (bf16[2,64,1,384]{3,1,2,0:T(8,128)(2,1)S(1)}, bf16[2,64,1,384]{3,1,2,0:T(8,128)(2,1)S(1)}, u32[]{:S(2)}, u32[]{:S(2)}) collective-permute-start(bf16[2,64,1,384]{3,1,2,0:T(8,128)(2,1)S(1)} %get-tuple-element.12), channel_id=1, source_target_pairs={{0,1},{1,2},{2,3},{3,4},{4,5},{5,6},{6,7},{7,8},{8,9},{9,10},{10,1... | collective-permute-start | bytes 294920 | tf_op jit(solution)/shard_map/ppermute | solution.py:16
  12.1 4.0 %collective-permute-start.1 = (bf16[2,64,1,384]{3,1,2,0:T(8,128)(2,1)S(1)}, bf16[2,64,1,384]{3,1,2,0:T(8,128)(2,1)S(1)}, u32[]{:S(2)}, u32[]{:S(2)}) collective-permute-start(bf16[2,64,1,384]{3,1,2,0:T(8,128)(2,1)S(1)} %get-tuple-element.13), channel_id=1, source_target_pairs={{1,0},{2,1},{3,2},{4,3},{5,4},{6,5},{7,6},{8,7},{9,8},{10,9},{11,1... | collective-permute-start | bytes 294920 | tf_op jit(solution)/shard_map/ppermute | solution.py:17
  12.7 0.7 copy-start.5
  28.0 10.3 %collective-permute-start.4 = (bf16[1,64,1,384]{3,1,2,0:T(8,128)(2,1)S(1)}, bf16[1,64,1,384]{3,1,2,0:T(8,128)(2,1)S(1)}, u32[]{:S(2)}, u32[]{:S(2)}) collective-permute-start(bf16[1,64,1,384]{3,1,2,0:T(8,128)(2,1)S(1)} %get-tuple-element.14), channel_id=1, source_target_pairs={{0,1},{1,2},{2,3},{3,4},{4,5},{5,6},{6,7},{7,8},{8,9},{9,10},{10,1... | collective-permute-start | bytes 147464 | tf_op jit(solution)/shard_map/ppermute | solution.py:16
  28.1 10.2 %collective-permute-start.5 = (bf16[1,64,1,384]{3,1,2,0:T(8,128)(2,1)S(1)}, bf16[1,64,1,384]{3,1,2,0:T(8,128)(2,1)S(1)}, u32[]{:S(2)}, u32[]{:S(2)}) collective-permute-start(bf16[1,64,1,384]{3,1,2,0:T(8,128)(2,1)S(1)} %get-tuple-element.15), channel_id=1, source_target_pairs={{1,0},{2,1},{3,2},{4,3},{5,4},{6,5},{7,6},{8,7},{9,8},{10,9},{11,1... | collective-permute-start | bytes 147464 | tf_op jit(solution)/shard_map/ppermute | solution.py:17
  32.9 9.3 %collective-permute-start.2 = (bf16[1,64,1,384]{3,1,2,0:T(8,128)(2,1)S(1)}, bf16[1,64,1,384]{3,1,2,0:T(8,128)(2,1)S(1)}, u32[]{:S(2)}, u32[]{:S(2)}) collective-permute-start(bf16[1,64,1,384]{3,1,2,0:T(8,128)(2,1)S(1)} %get-tuple-element.16), channel_id=1, source_target_pairs={{0,1},{1,2},{2,3},{3,4},{4,5},{5,6},{6,7},{7,8},{8,9},{9,10},{10,1... | collective-permute-start | bytes 147464 | tf_op jit(solution)/shard_map/ppermute | solution.py:16
  32.9 9.3 %collective-permute-start.3 = (bf16[1,64,1,384]{3,1,2,0:T(8,128)(2,1)S(1)}, bf16[1,64,1,384]{3,1,2,0:T(8,128)(2,1)S(1)}, u32[]{:S(2)}, u32[]{:S(2)}) collective-permute-start(bf16[1,64,1,384]{3,1,2,0:T(8,128)(2,1)S(1)} %get-tuple-element.17), channel_id=1, source_target_pairs={{1,0},{2,1},{3,2},{4,3},{5,4},{6,5},{7,6},{8,7},{9,8},{10,9},{11,1... | collective-permute-start | bytes 147464 | tf_op jit(solution)/shard_map/ppermute | solution.py:17
  44.5 1.4 copy-start.3
Sparse Core Ops, SparseCore 0:
  60.9 254.3 all-reduce.7
where the time goes:
time: 326 us; the launch traced here: 325 us
  waiting for transfers between devices  250 us (77%)
  matrix products  36 us (11%)
  between operations  14.5 us (4%)
  starting transfers between devices  13.7 us (4%)
  other arithmetic  7.25 us (2%)
  local copies, waits for them, and re-layouts  3.62 us (1%)
    psum x1, waiting for transfers between devices, per_device(): first, second = lax.psum((first, second), ('dp', 'lon'))  248 us
    dot_general x18, matrix products, stencil_adjoint(): jnp.einsum('oc,boij->bcij', taps[p, q], source[:, :, 2 - p:2 - p + column...  22.2 us
    ppermute x3, starting transfers between devices, extended(): after = lax.ppermute(first, axis, down)  10.4 us
    dot_general x18, matrix products, kernel_term(): jnp.einsum('boij,bcij->oc', source, padded[:, :, p:p + columns, q:q + lat...  9.32 us
  transfers between devices with their start and end apart: 7, of which 3 were waited for; matrix products, arithmetic and copies ran while one was open for 3% of the time, Pallas kernels for 0%

commit v1 on v0

--- a/solution.py
+++ b/solution.py
@@ -111,7 +111,7 @@
         cotangent.astype(jnp.float32) + stencil_adjoint(delta_pad, delta_scaled, kernel_first)
     ).astype(jnp.bfloat16)
     first = kernel_term(delta, delta_scaled[:, :, 1:-1, 1:-1], input_pad)
-    first, second = lax.psum((first, second), ("dp", "lon"))
+    first, second = lax.psum(lax.psum((first, second), "dp"), "lon")
     counted = (
         float(fields.shape[0] * lax.axis_size("dp"))
         * float(fields.shape[2] * lax.axis_size("lon"))

time: 326 us -> 411 us (1.26)
  waiting for transfers between devices: 250 us -> 333 us
    psum x1 -> x2, waiting for transfers between devices: 248 us -> 330 us  [per_device(): first, second = lax.psum(lax.psum((first, second), 'dp'), 'lon')]
  transfers between devices with their start and end apart: 7 -> 8, of which waited for: 3 -> 4; matrix products, arithmetic and copies ran while one was open for 3% -> 4% of each run, Pallas kernels for 0% -> 0%
where the time goes in v1:
time: 411 us; the launch traced here: 410 us
  waiting for transfers between devices  333 us (81%)
  matrix products  37.4 us (9%)
  between operations  14.5 us (4%)
  starting transfers between devices  14.1 us (3%)
  other arithmetic  7.23 us (2%)
    psum x2, waiting for transfers between devices, per_device(): first, second = lax.psum(lax.psum((first, second), 'dp'), 'lon')  330 us
    dot_general x18, matrix products, stencil_adjoint(): jnp.einsum('oc,boij->bcij', taps[p, q], source[:, :, 2 - p:2 - p + column...  23.6 us
    ppermute x3, starting transfers between devices, extended(): after = lax.ppermute(first, axis, down)  10.4 us
    dot_general x18, matrix products, kernel_term(): jnp.einsum('boij,bcij->oc', source, padded[:, :, p:p + columns, q:q + lat...  9.33 us
  transfers between devices with their start and end apart: 8, of which 4 were waited for; matrix products, arithmetic and copies ran while one was open for 4% of the time, Pallas kernels for 0%

profile of v1, /device:TPU:1, one launch (start us, length us, event | category | flops | bytes accessed | tf_op | source)
XLA Modules:
  0.0 409.8 jit_solution(15383977087420846891)
XLA Ops:
  7.2 1.4 copy_dynamic-update-slice_fusion
  9.0 3.1 collective-permute-start
  13.7 2.4 collective-permute-done.1
  16.6 0.4 fusion.53
  17.0 0.4 fusion.56
  17.5 0.4 fusion.59
  17.9 0.4 fusion.62
  18.3 0.4 fusion.65
  18.8 0.4 fusion.68
  19.6 1.2 multiply_convert_fusion.2
  21.1 0.6 multiply_convert_fusion.1
  21.7 0.4 fusion.38
  22.2 0.4 fusion.39
  23.0 0.4 fusion.41
  23.5 0.4 fusion.42
  24.8 1.6 fusion.7
  28.3 4.7 %collective-permute-start.5 = (bf16[1,64,1,384]{3,1,2,0:T(8,128)(2,1)S(1)}, bf16[1,64,1,384]{3,1,2,0:T(8,128)(2,1)S(1)}, u32[]{:S(2)}, u32[]{:S(2)}) collective-permute-start(bf16[1,64,1,384]{3,1,2,0:T(8,128)(2,1)S(1)} %get-tuple-element.17), channel_id=1, source_target_pairs={{1,0},{2,1},{3,2},{4,3},{5,4},{6,5},{7,6},{8,7},{9,8},{10,9},{11,1... | collective-permute-start | bytes 147464 | tf_op jit(solution)/shard_map/ppermute | solution.py:17
  33.1 5.4 %collective-permute-start.3 = (bf16[1,64,1,384]{3,1,2,0:T(8,128)(2,1)S(1)}, bf16[1,64,1,384]{3,1,2,0:T(8,128)(2,1)S(1)}, u32[]{:S(2)}, u32[]{:S(2)}) collective-permute-start(bf16[1,64,1,384]{3,1,2,0:T(8,128)(2,1)S(1)} %get-tuple-element.19), channel_id=1, source_target_pairs={{1,0},{2,1},{3,2},{4,3},{5,4},{6,5},{7,6},{8,7},{9,8},{10,9},{11,1... | collective-permute-start | bytes 147464 | tf_op jit(solution)/shard_map/ppermute | solution.py:17
  38.5 0.7 select_maximum_fusion
  39.2 0.5 convolution_bitcast_fusion.3
  40.1 0.4 convolution_bitcast_fusion.2
  40.5 0.7 convolution_bitcast_fusion
  41.2 0.4 convolution_bitcast_fusion.8
  41.7 0.7 convolution_bitcast_fusion.6
  42.4 0.9 multiply_convert_fusion
  43.3 0.7 convolution_bitcast_fusion.11
  44.0 0.7 convolution_bitcast_fusion.15
  44.7 0.7 convolution_bitcast_fusion.17
  45.3 0.7 convolution_bitcast_fusion.9
  46.0 1.6 fusion.29
  47.7 1.6 fusion.30
  49.3 1.6 fusion.31
  50.9 1.7 fusion.32
  52.5 1.5 fusion.33
  54.1 0.5 convolution_bitcast_fusion.1
  54.6 0.5 convolution_bitcast_fusion.7
  55.1 0.7 pad_maximum_fusion.6
  55.8 0.5 convolution_bitcast_fusion.10
  56.3 0.5 convolution_bitcast_fusion.16
  56.8 0.7 pad_maximum_fusion.5
  57.8 2.3 fusion.34
  60.2 2.4 fusion.35
  62.6 71.2 %all-reduce.12.cloned.1.call-done = (f32[3,3,64,64]{3,2,1,0:T(8,128)}, f32[3,3,64,64]{3,2,1,0:T(8,128)}) async-done(((f32[3,3,64,64]{3,2,1,0:T(8,128)}, f32[3,3,64,64]{3,2,1,0:T(8,128)}), (f32[3,3,64,64]{3,2,1,0:T(8,128)}, f32[3,3,64,64]{3,2,1,0:T(8,128)})) %all-reduce.12.cloned.1.call-update) | async-done | bytes 294928 | tf_op jit(solution)/shard_map/psum | solution.py:114
  133.9 5.4 %fusion.8 = bf16[1,64,16,384]{3,1,2,0:T(8,128)(2,1)S(1)} fusion(f32[16,384,64]{1,2,0:T(8,128)} %fusion.29, f32[16,384,64]{1,2,0:T(8,128)} %fusion.30, f32[16,384,64]{1,2,0:T(8,128)} %fusion.31, f32[16,384,64]{1,2,0:T(8,128)S(1)} %fusion.47, f32[16,384,64]{1,2,0:T(8,128)} %fusion.32, f32[16,384,64]{1,2,0:T(8,128)} %fusion.33, f32[16,384,64]{1,2,0:T(8,128)} %fusion.35, ...), kind=kOutput, calls=%fused_computation.16 | convolution fusion | flops 54657024 | bytes 14958592 | tf_op jit(solution)/shard_map/oc,boij->bcij/dot_general | solution.py:64
  139.2 1.3 copy.38
  140.6 259.0 %all-reduce.10.cloned.1.call-done = (f32[3,3,64,64]{3,2,1,0:T(8,128)}, f32[3,3,64,64]{3,2,1,0:T(8,128)}) async-done(((f32[3,3,64,64]{3,2,1,0:T(8,128)}, f32[3,3,64,64]{3,2,1,0:T(8,128)}), (f32[3,3,64,64]{3,2,1,0:T(8,128)}, f32[3,3,64,64]{3,2,1,0:T(8,128)})) %all-reduce.10.cloned.1.call-update) | async-done | bytes 294928 | tf_op jit(solution)/shard_map/psum | solution.py:114
  399.6 1.7 multiply_convert_fusion.3
  401.3 1.7 multiply_convert_fusion.4
  (47 shorter events, 7.0 us)
Async XLA Ops:
  7.2 5.2 %copy-start.1 = (bf16[1,64,16,384]{3,2,1,0:T(8,128)(2,1)S(1)}, bf16[1,64,16,384]{3,2,1,0:T(8,128)(2,1)}, u32[]{:S(2)}) copy-start(bf16[1,64,16,384]{3,2,1,0:T(8,128)(2,1)} %param.5) | copy-start | bytes 2359300
  7.2 1.5 copy-start
  7.2 5.2 %copy-start.2 = (bf16[3,3,64,64]{3,2,1,0:T(8,128)(2,1)S(1)}, bf16[3,3,64,64]{3,2,1,0:T(8,128)(2,1)}, u32[]{:S(2)}) copy-start(bf16[3,3,64,64]{3,2,1,0:T(8,128)(2,1)} %param.7) | copy-start | bytes 221188
  7.2 126.6 %all-reduce.12.cloned.1.call-start = ((), (), s32[]{:S(2)}) async-start(), calls=%async_computation.1 | async-start | bytes 1179648 | tf_op jit(solution)/shard_map/psum | solution.py:114
  8.9 3.8 copy-start.4
  9.0 4.7 %collective-permute-start = (bf16[2,64,1,384]{3,1,2,0:T(8,128)(2,1)S(1)}, bf16[2,64,1,384]{3,1,2,0:T(8,128)(2,1)S(1)}, u32[]{:S(2)}, u32[]{:S(2)}) collective-permute-start(bf16[2,64,1,384]{3,1,2,0:T(8,128)(2,1)S(1)} %get-tuple-element.14), channel_id=1, source_target_pairs={{0,1},{1,2},{2,3},{3,4},{4,5},{5,6},{6,7},{7,8},{8,9},{9,10},{10,1... | collective-permute-start | bytes 294920 | tf_op jit(solution)/shard_map/ppermute | solution.py:16
  12.1 4.0 collective-permute-start.1
  12.7 0.7 copy-start.5
  28.0 10.5 %collective-permute-start.4 = (bf16[1,64,1,384]{3,1,2,0:T(8,128)(2,1)S(1)}, bf16[1,64,1,384]{3,1,2,0:T(8,128)(2,1)S(1)}, u32[]{:S(2)}, u32[]{:S(2)}) collective-permute-start(bf16[1,64,1,384]{3,1,2,0:T(8,128)(2,1)S(1)} %get-tuple-element.16), channel_id=1, source_target_pairs={{0,1},{1,2},{2,3},{3,4},{4,5},{5,6},{6,7},{7,8},{8,9},{9,10},{10,1... | collective-permute-start | bytes 147464 | tf_op jit(solution)/shard_map/ppermute | solution.py:16
  28.3 10.2 %collective-permute-start.5 = (bf16[1,64,1,384]{3,1,2,0:T(8,128)(2,1)S(1)}, bf16[1,64,1,384]{3,1,2,0:T(8,128)(2,1)S(1)}, u32[]{:S(2)}, u32[]{:S(2)}) collective-permute-start(bf16[1,64,1,384]{3,1,2,0:T(8,128)(2,1)S(1)} %get-tuple-element.17), channel_id=1, source_target_pairs={{1,0},{2,1},{3,2},{4,3},{5,4},{6,5},{7,6},{8,7},{9,8},{10,9},{11,1... | collective-permute-start | bytes 147464 | tf_op jit(solution)/shard_map/ppermute | solution.py:17
  33.0 9.3 %collective-permute-start.2 = (bf16[1,64,1,384]{3,1,2,0:T(8,128)(2,1)S(1)}, bf16[1,64,1,384]{3,1,2,0:T(8,128)(2,1)S(1)}, u32[]{:S(2)}, u32[]{:S(2)}) collective-permute-start(bf16[1,64,1,384]{3,1,2,0:T(8,128)(2,1)S(1)} %get-tuple-element.18), channel_id=1, source_target_pairs={{0,1},{1,2},{2,3},{3,4},{4,5},{5,6},{6,7},{7,8},{8,9},{9,10},{10,1... | collective-permute-start | bytes 147464 | tf_op jit(solution)/shard_map/ppermute | solution.py:16
  33.1 9.3 %collective-permute-start.3 = (bf16[1,64,1,384]{3,1,2,0:T(8,128)(2,1)S(1)}, bf16[1,64,1,384]{3,1,2,0:T(8,128)(2,1)S(1)}, u32[]{:S(2)}, u32[]{:S(2)}) collective-permute-start(bf16[1,64,1,384]{3,1,2,0:T(8,128)(2,1)S(1)} %get-tuple-element.19), channel_id=1, source_target_pairs={{1,0},{2,1},{3,2},{4,3},{5,4},{6,5},{7,6},{8,7},{9,8},{10,9},{11,1... | collective-permute-start | bytes 147464 | tf_op jit(solution)/shard_map/ppermute | solution.py:17
  44.6 1.4 copy-start.3
  57.6 342.1 %all-reduce.10.cloned.1.call-start = ((), (), s32[]{:S(2)}) async-start(), calls=%async_computation | async-start | bytes 1179648 | tf_op jit(solution)/shard_map/psum | solution.py:114
Sparse Core Ops, SparseCore 0:
  57.7 76.1 all-reduce.11
  136.5 263.0 all-reduce.9
